TPU v7x, 256 devices: a whole 4x4x8 slice. The times are simulated.
256 devices in a mesh: row: 16 (over x_lo, z), col: 16 (over x_hi, y, core).
Axes of the slice: x: 4 (x_hi: 2, x_lo: 2; x = x_hi * 2 + x_lo), y: 4, z: 8, core: 2. Of those that a mesh axis runs over, the one named last changes fastest.
Arguments:
- tensor: bfloat16 [4096, 2048, 128], P('row', 'col'), may hold values from -96 to 96
- factor_a: float32 [4096, 128], P(('row', 'col')), may hold values from -4.5 to 4.5
- factor_b: float32 [2048, 128], P(('col', 'row')), may hold values from -4.5 to 4.5
- factor_c: float32 [128, 128], replicated, may hold values from -4.5 to 4.5
Outputs:
- new_a: float32 [4096, 128], P(('row', 'col'))
- new_b: float32 [2048, 128], P(('col', 'row'))
- new_c: float32 [128, 128], replicated
All inputs are finite; a program needn't handle non-finite values.
Results may differ from a plain program's by a relative error of at most 0.01.
Values may be sent and summed in bfloat16 or wider, within the bound.
A program may use at most 128 MiB of HBM per device.

v0:
```python
import jax
import jax.numpy as jnp
from jax import lax
from jax.sharding import PartitionSpec as P

STEPS = 2
damping = 0.9
scaling = 0.25
epsilon = 1e-06


def column_squares(values16):
    return jnp.sum(jnp.square(values16.astype(jnp.float32)), axis=0)


def local_terms(block, tile_a, tile_b, c16):
    rows_i, rows_j, depth = block.shape
    rank = tile_a.shape[1]
    pairs = (
        tile_a.astype(jnp.float32)[:, None, :] * tile_b.astype(jnp.float32)[None, :, :]
    ).astype(jnp.bfloat16)
    pairs = pairs.reshape(rows_i * rows_j, rank)
    model = jnp.dot(pairs, c16.T, preferred_element_type=jnp.float32)
    resid = (block.reshape(rows_i * rows_j, depth).astype(jnp.float32) - model).astype(jnp.bfloat16)
    along = jnp.dot(resid, c16, preferred_element_type=jnp.float32).reshape(rows_i, rows_j, rank)
    grad_a = jnp.sum(along * tile_b.astype(jnp.float32)[None, :, :], axis=1)
    grad_b = jnp.sum(along * tile_a.astype(jnp.float32)[:, None, :], axis=0)
    grad_c = lax.dot_general(
        resid, pairs, (((0,), (0,)), ((), ())), preferred_element_type=jnp.float32
    )
    return (grad_a, grad_b, grad_c)


def local(tensor, factor_a, factor_b, factor_c):
    own_a, own_b, third = (factor_a, factor_b, factor_c)
    for step in range(STEPS):
        a_mine16 = own_a.astype(jnp.bfloat16)
        b_mine16 = own_b.astype(jnp.bfloat16)
        tile_a = lax.all_gather(a_mine16, "col", axis=0, tiled=True)
        tile_b = lax.all_gather(b_mine16, "row", axis=0, tiled=True)
        norm_a, norm_b = lax.psum(
            (column_squares(a_mine16), column_squares(b_mine16)), ("row", "col")
        )
        c16 = third.astype(jnp.bfloat16)
        norm_c = column_squares(c16)
        step_a = scaling / (norm_b * norm_c + epsilon)
        step_b = scaling / (norm_a * norm_c + epsilon)
        step_c = scaling / (norm_a * norm_b + epsilon)
        grad_a, grad_b, grad_c = local_terms(tensor, tile_a, tile_b, c16)
        grad_a = lax.psum_scatter(
            grad_a.astype(jnp.bfloat16), "col", scatter_dimension=0, tiled=True
        ).astype(jnp.float32)
        grad_b = lax.psum_scatter(
            grad_b.astype(jnp.bfloat16), "row", scatter_dimension=0, tiled=True
        ).astype(jnp.float32)
        own_a = damping * own_a + step_a * grad_a
        own_b = damping * own_b + step_b * grad_b
        grad_c = lax.psum(grad_c, ("row", "col"))
        third = damping * third + step_c * grad_c
    return (own_a, own_b, third)


def solution(mesh):
    return jax.shard_map(
        local,
        mesh=mesh,
        in_specs=(P("row", "col", None), P(("row", "col"), None), P(("col", "row"), None), P()),
        out_specs=(P(("row", "col"), None), P(("col", "row"), None), P()),
        check_vma=False,
    )
```

profile of v0, /device:TPU:1, one launch (start us, length us, event | category | flops | bytes accessed | tf_op | source)
XLA Modules:
  0.0 663.4 jit_solution(11993279583761159699)
XLA Ops:
  8.0 0.0 copy-start.2
  8.0 0.0 all-reduce.7.cloned.1.call-start
  8.1 0.7 multiply_reduce_fusion.9
  8.8 0.7 multiply_reduce_fusion.7
  9.5 30.3 %all_gather.13 = bf16[128,128]{1,0:T(8,128)(2,1)S(1)} all-gather(bf16[8,128]{1,0:T(8,128)(2,1)S(1)} %get-tuple-element.14), channel_id=1, replica_groups=mesh['row'=16,'col'=16] {'row'}, dimensions={0}, use_global_device_ids=true | all-gather | bytes 34816 | tf_op jit(solution)/shard_map/all_gather | solution.py:40
  39.8 31.7 %all_gather.12 = bf16[256,128]{1,0:T(8,128)(2,1)S(1)} all-gather(bf16[16,128]{1,0:T(8,128)(2,1)S(1)} %get-tuple-element.16), channel_id=1, replica_groups=mesh['row'=16,'col'=16] {'col'}, dimensions={0}, use_global_device_ids=true | all-gather | bytes 69632 | tf_op jit(solution)/shard_map/all_gather | solution.py:39
  71.5 5.6 multiply_convert_fusion.1
  77.1 0.0 copy-done.2
  77.1 8.1 %fusion.1 = bf16[32768,128]{1,0:T(8,128)(2,1)S(1)} fusion(bf16[32768,128]{1,0:T(8,128)(2,1)} %bitcast.21, bf16[32768,128]{1,0:T(8,128)(2,1)} %bitcast.25, f32[128,128]{1,0:T(8,128)S(1)} %copy-done.2), kind=kOutput, calls=%fused_computation.3 | convolution fusion | flops 1086341120 | bytes 25231360 | tf_op jit(solution)/shard_map/dot_general | solution.py:23
  85.2 0.0 copy-start
  85.2 3.2 copy-done
  88.5 6.4 fusion.11
  94.8 0.0 all-reduce.7.cloned.1.call-update
  94.9 0.0 reduce-scatter.3.cloned.1.call-start
  94.9 12.1 %multiply_reduce_fusion.3 = (bf16[256,128]{1,0:T(8,128)(2,1)}, f32[32768,128]{1,0:T(8,128)}) fusion(f32[128,128]{1,0:T(8,128)S(1)} %convert_element_type.111, bf16[32768,128]{1,0:T(8,128)(2,1)} %copy-done, f32[128,128]{1,0:T(8,128)S(1)} %copy-done.2), kind=kOutput, calls=%fused_computation.8 | convolution fusion | flops 1082114048 | bytes 25362432 | tf_op jit(solution)/shard_map/dot_general | solution.py:25
  107.0 0.0 reduce-scatter.3.cloned.1.call-update
  107.0 0.0 all-reduce.9.cloned.1.call-start
  107.1 0.0 copy-start.7
  107.1 0.0 copy-start.5
  107.1 0.0 copy-start.4
  107.1 7.3 %multiply_reduce_fusion.2 = bf16[128,128]{1,0:T(8,128)(2,1)S(1)} fusion(f32[256,128,128]{2,1,0:T(8,128)} %bitcast.23, f32[256,128]{1,0:T(8,128)S(1)} %convert_element_type.110), kind=kLoop, calls=%fused_computation.7 | loop fusion | flops 8372224 | bytes 16941056 | tf_op jit(solution)/shard_map/reduce_sum | solution.py:27
  114.5 46.3 %all-reduce = bf16[128,128]{1,0:T(8,128)(2,1)S(1)} all-reduce(bf16[128,128]{1,0:T(8,128)(2,1)S(1)} %multiply_reduce_fusion.2), channel_id=3, replica_groups=mesh['row'=16,'col'=16] {'row'}, use_global_device_ids=true, to_apply=%region_8.0.clone | all-reduce | flops 16384 | bytes 65536
  160.8 0.0 copy-done.7
  160.8 0.6 dynamic-slice
  162.0 84.4 %all-reduce.3 = (f32[128]{0:T(128)S(1)}, f32[128]{0:T(128)S(1)}) all-reduce(f32[128]{0:T(128)S(1)} %get-tuple-element.15, f32[128]{0:T(128)S(1)} %get-tuple-element.13), channel_id=1, replica_groups=mesh['row'=16,'col'=16] {'row','col'}, use_global_device_ids=true, to_apply=%region_6.0 | all-reduce | flops 256 | bytes 2048 | tf_op jit(solution)/shard_map/psum | solution.py:41
  246.4 81.7 %all-reduce.7.cloned.1.call-done = f32[128,128]{1,0:T(8,128)} async-done(((f32[128,128]{1,0:T(8,128)}), f32[128,128]{1,0:T(8,128)}) %all-reduce.7.cloned.1.call-update) | async-done | bytes 65552 | tf_op jit(solution)/shard_map/psum | solution.py:58
  328.1 0.9 multiply_reduce_fusion.4
  329.0 0.0 copy-done.5
  329.1 24.4 %all_gather.15 = bf16[128,128]{1,0:T(8,128)(2,1)S(1)} all-gather(bf16[8,128]{1,0:T(8,128)(2,1)S(1)} %get-tuple-element.12), channel_id=1, replica_groups=mesh['row'=16,'col'=16] {'row'}, dimensions={0}, use_global_device_ids=true | all-gather | bytes 34816 | tf_op jit(solution)/shard_map/all_gather | solution.py:40
  353.5 0.0 reduce-scatter.3.cloned.1.call-done
  353.5 0.0 copy-done.4
  353.5 0.7 multiply_reduce_fusion.6
  354.2 28.8 %all_gather.14 = bf16[256,128]{1,0:T(8,128)(2,1)S(1)} all-gather(bf16[16,128]{1,0:T(8,128)(2,1)S(1)} %get-tuple-element.10), channel_id=1, replica_groups=mesh['row'=16,'col'=16] {'col'}, dimensions={0}, use_global_device_ids=true | all-gather | bytes 69632 | tf_op jit(solution)/shard_map/all_gather | solution.py:39
  383.0 5.6 multiply_convert_fusion
  388.6 8.1 %fusion = bf16[32768,128]{1,0:T(8,128)(2,1)S(1)} fusion(bf16[32768,128]{1,0:T(8,128)(2,1)} %bitcast.19, bf16[128,128]{1,0:T(8,128)(2,1)S(1)} %get-tuple-element.8, bf16[32768,128]{1,0:T(8,128)(2,1)} %bitcast.26), kind=kOutput, calls=%fused_computation.1 | convolution fusion | flops 1086324736 | bytes 25198592 | tf_op jit(solution)/shard_map/dot_general | solution.py:23
  396.7 0.0 copy-start.1
  396.8 3.2 copy-done.1
  400.0 6.4 fusion.12
  406.4 12.1 %multiply_reduce_fusion.1 = (bf16[256,128]{1,0:T(8,128)(2,1)}, f32[32768,128]{1,0:T(8,128)}) fusion(f32[128,128]{1,0:T(8,128)S(1)} %convert_element_type.126, bf16[32768,128]{1,0:T(8,128)(2,1)} %copy-done.1, bf16[128,128]{1,0:T(8,128)(2,1)S(1)} %get-tuple-element.8), kind=kOutput, calls=%fused_computation.5 | convolution fusion | flops 1082097664 | bytes 25329664 | tf_op jit(solution)/shard_map/dot_general | solution.py:25
  418.4 0.0 all-reduce.9.cloned.1.call-update
  418.4 0.0 reduce-scatter.5.cloned.1.call-start
  418.5 0.0 copy-start.3
  418.5 0.0 copy-start.6
  418.5 7.3 %multiply_reduce_fusion = bf16[128,128]{1,0:T(8,128)(2,1)S(1)} fusion(f32[256,128,128]{2,1,0:T(8,128)} %bitcast.24, f32[256,128]{1,0:T(8,128)S(1)} %convert_element_type.125), kind=kLoop, calls=%fused_computation.4 | loop fusion | flops 8372224 | bytes 16941056 | tf_op jit(solution)/shard_map/reduce_sum | solution.py:27
  425.8 47.7 %all-reduce.1 = bf16[128,128]{1,0:T(8,128)(2,1)S(1)} all-reduce(bf16[128,128]{1,0:T(8,128)(2,1)S(1)} %multiply_reduce_fusion), channel_id=5, replica_groups=mesh['row'=16,'col'=16] {'row'}, use_global_device_ids=true, to_apply=%region_18.0.clone | all-reduce | flops 16384 | bytes 65536
  473.5 86.2 %all-reduce.2 = (f32[128]{0:T(128)S(1)}, f32[128]{0:T(128)S(1)}) all-reduce(f32[128]{0:T(128)S(1)} %get-tuple-element.11, f32[128]{0:T(128)S(1)} %get-tuple-element.9), channel_id=1, replica_groups=mesh['row'=16,'col'=16] {'row','col'}, use_global_device_ids=true, to_apply=%region_10.0 | all-reduce | flops 256 | bytes 2048 | tf_op jit(solution)/shard_map/psum | solution.py:41
  559.7 0.6 multiply_add_fusion.4
  560.3 0.0 reduce-scatter.5.cloned.1.call-update
  560.3 92.8 %all-reduce.9.cloned.1.call-done = f32[128,128]{1,0:T(8,128)} async-done(((f32[128,128]{1,0:T(8,128)}), f32[128,128]{1,0:T(8,128)}) %all-reduce.9.cloned.1.call-update) | async-done | bytes 65552 | tf_op jit(solution)/shard_map/psum | solution.py:58
  653.2 0.0 copy-done.3
  653.2 1.5 multiply_add_fusion
  654.6 0.0 reduce-scatter.5.cloned.1.call-done
  654.6 0.0 copy-done.6
  654.6 1.3 multiply_add_fusion.2
  (8 shorter events, 0.1 us)
Async XLA Ops:
  8.0 69.1 %copy-start.2 = (f32[128,128]{1,0:T(8,128)S(1)}, f32[128,128]{1,0:T(8,128)}, u32[]{:S(2)}) copy-start(f32[128,128]{1,0:T(8,128)} %param.7) | copy-start | bytes 196612
  8.0 320.1 %all-reduce.7.cloned.1.call-start = ((), (), s32[]{:S(2)}) async-start(), calls=%async_computation.3 | async-start | bytes 131072 | tf_op jit(solution)/shard_map/psum | solution.py:58
  85.2 3.2 copy-start
  94.9 258.6 %reduce-scatter.3.cloned.1.call-start = ((), (), s32[]{:S(2)}) async-start(), calls=%async_computation.2 | async-start | bytes 69632 | tf_op jit(solution)/shard_map/reduce_scatter | solution.py:50
  107.0 546.1 %all-reduce.9.cloned.1.call-start = ((), (), s32[]{:S(2)}) async-start(), calls=%async_computation.5 | async-start | bytes 131072 | tf_op jit(solution)/shard_map/psum | solution.py:58
  107.1 53.7 %copy-start.7 = (u32[256]{0:T(256)S(1)}, u32[256]{0:T(256)}, u32[]{:S(2)}) copy-start(u32[256]{0:T(256)} %constant.14) | copy-start | bytes 3076
  107.1 221.9 %copy-start.5 = (f32[8,128]{1,0:T(8,128)S(1)}, f32[8,128]{1,0:T(8,128)}, u32[]{:S(2)}) copy-start(f32[8,128]{1,0:T(8,128)} %param.6) | copy-start | bytes 12292
  107.1 246.4 %copy-start.4 = (f32[16,128]{1,0:T(8,128)S(1)}, f32[16,128]{1,0:T(8,128)}, u32[]{:S(2)}) copy-start(f32[16,128]{1,0:T(8,128)} %param.5) | copy-start | bytes 24580
  396.7 3.2 copy-start.1
  418.4 236.2 %reduce-scatter.5.cloned.1.call-start = ((), (), s32[]{:S(2)}) async-start(), calls=%async_computation.4 | async-start | bytes 69632 | tf_op jit(solution)/shard_map/reduce_scatter | solution.py:50
  418.5 234.7 %copy-start.3 = (f32[128,128]{1,0:T(8,128)S(1)}, f32[128,128]{1,0:T(8,128)}, u32[]{:S(2)}) copy-start(f32[128,128]{1,0:T(8,128)} %all-reduce.7.cloned.1.call-done) | copy-start | bytes 196612
  418.5 236.1 %copy-start.6 = (bf16[16,128]{1,0:T(8,128)(2,1)S(1)}, bf16[16,128]{1,0:T(8,128)(2,1)}, u32[]{:S(2)}) copy-start(bf16[16,128]{1,0:T(8,128)(2,1)} %reduce-scatter.3.cloned.1.call-done) | copy-start | bytes 12292
Sparse Core Ops, SparseCore 0:
  95.0 233.1 all-reduce.6
  418.6 234.5 all-reduce.8
Sparse Core Ops, SparseCore 1:
  107.1 58.3 reduce-scatter.2
  560.4 60.9 reduce-scatter.4
where the time goes:
time: 664 us; the launch traced here: 663 us
  blocking collectives  380 us (57%)
  waiting for transfers between devices  175 us (26%)
  matrix products  53.2 us (8%)
  other arithmetic  32.4 us (5%)
  between operations  16.3 us (2%)
  local copies, waits for them, and re-layouts  7.04 us (1%)
    psum x2, waiting for transfers between devices, local(): grad_c = lax.psum(grad_c, ('row', 'col'))  175 us
    psum x2, blocking collectives, local(): lax.psum((column_squares(a_mine16), column_squares(b_mine16)), ('row', 'c...  171 us
    unnamed x2, blocking collectives  94 us
    all_gather x2, blocking collectives, local(): tile_a = lax.all_gather(a_mine16, 'col', axis=0, tiled=True)  60.5 us
    all_gather x2, blocking collectives, local(): tile_b = lax.all_gather(b_mine16, 'row', axis=0, tiled=True)  54.7 us
    dot_general x2, matrix products, local_terms(): jnp.dot(resid, c16, preferred_element_type=jnp.float32)  24.1 us
    dot_general x2, matrix products, local_terms(): model = jnp.dot(pairs, c16.T, preferred_element_type=jnp.float32)  16.2 us
    reduce_sum x2, other arithmetic, local_terms(): grad_b = jnp.sum(along * tile_a.astype(jnp.float32)[:, None, :], axis=0)  14.7 us
  transfers between devices with their start and end apart: 4, of which 2 were waited for; matrix products, arithmetic and copies ran while one was open for 5% of the time, Pallas kernels for 0%

commit v1 on v0

--- a/solution.py
+++ b/solution.py
@@ -37,7 +37,9 @@
         a_mine16 = own_a.astype(jnp.bfloat16)
         b_mine16 = own_b.astype(jnp.bfloat16)
         tile_a = lax.all_gather(a_mine16, "col", axis=0, tiled=True)
-        tile_b = lax.all_gather(b_mine16, "row", axis=0, tiled=True)
+        tile_b = jnp.concatenate(
+            lax.all_to_all(jnp.stack([b_mine16] * lax.axis_size("row")), "row", 0, 0), axis=0
+        )
         norm_a, norm_b = lax.psum(
             (column_squares(a_mine16), column_squares(b_mine16)), ("row", "col")
         )

time: 664 us -> 785 us (1.18)
  waiting for transfers between devices: 175 us -> 352 us
  blocking collectives: 380 us -> 308 us
  starting transfers between devices: 0.17 us -> 13.7 us
    psum x2, waiting for transfers between devices: 175 us -> 279 us  [local(): grad_c = lax.psum(grad_c, ('row', 'col'))]
    reduce_scatter x2, waiting for transfers between devices: 0.02 us -> 65.4 us  [local(): lax.psum_scatter(grad_a.astype(jnp.bfloat16), 'col', scatter_dimension=0,...]
    all_gather x2 -> x0, blocking collectives: 54.7 us -> none  [local(): tile_b = lax.all_gather(b_mine16, 'row', axis=0, tiled=True)]
    all_gather x2, blocking collectives: 60.5 us -> 45.8 us  [local(): tile_a = lax.all_gather(a_mine16, 'col', axis=0, tiled=True)]
    all_to_all x0 -> x2, starting transfers between devices: none -> 13.5 us  [local(): lax.all_to_all(jnp.stack([b_mine16] * lax.axis_size('row')), 'row', 0, 0)]
  transfers between devices with their start and end apart: 4 -> 6, of which waited for: 2 -> 4; matrix products, arithmetic and copies ran while one was open for 5% -> 2% of each run, Pallas kernels for 0% -> 0%
where the time goes in v1:
time: 785 us; the launch traced here: 784 us
  waiting for transfers between devices  352 us (45%)
  blocking collectives  308 us (39%)
  matrix products  53.1 us (7%)
  other arithmetic  32.3 us (4%)
  between operations  16.3 us (2%)
  starting transfers between devices  13.7 us (2%)
  local copies, waits for them, and re-layouts  8.94 us (1%)
    psum x2, waiting for transfers between devices, local(): grad_c = lax.psum(grad_c, ('row', 'col'))  279 us
    psum x2, blocking collectives, local(): lax.psum((column_squares(a_mine16), column_squares(b_mine16)), ('row', 'c...  164 us
    unnamed x2, blocking collectives  97.9 us
    reduce_scatter x2, waiting for transfers between devices, local(): lax.psum_scatter(grad_a.astype(jnp.bfloat16), 'col', scatter_dimension=0,...  65.4 us
    all_gather x2, blocking collectives, local(): tile_a = lax.all_gather(a_mine16, 'col', axis=0, tiled=True)  45.8 us
    dot_general x2, matrix products, local_terms(): jnp.dot(resid, c16, preferred_element_type=jnp.float32)  24.1 us
    dot_general x2, matrix products, local_terms(): model = jnp.dot(pairs, c16.T, preferred_element_type=jnp.float32)  16.2 us
  transfers between devices with their start and end apart: 6, of which 4 were waited for; matrix products, arithmetic and copies ran while one was open for 2% of the time, Pallas kernels for 0%

profile of v1, /device:TPU:1, one launch (start us, length us, event | category | flops | bytes accessed | tf_op | source)
XLA Modules:
  0.0 784.1 jit_solution(3703987832898902721)
XLA Ops:
  8.0 0.0 copy-start.2
  8.0 0.7 multiply_reduce_fusion.9
  8.7 0.6 stack.4
  9.4 10.0 %all-to-all-start = ((bf16[16,8,128]{2,1,0:T(8,128)(2,1)}), bf16[16,8,128]{2,1,0:T(8,128)(2,1)S(1)}, u32[]{:S(2)}, u32[]{:S(2)}) async-start(bf16[16,8,128]{2,1,0:T(8,128)(2,1)} %stack.4), calls=%async_computation | async-start | bytes 65536 | tf_op jit(solution)/shard_map/all_to_all | solution.py:41
  19.4 0.0 all-reduce.7.cloned.1.call-start
  19.5 0.7 multiply_reduce_fusion.7
  20.2 77.5 %all-reduce.3 = (f32[128]{0:T(128)S(1)}, f32[128]{0:T(128)S(1)}) all-reduce(f32[128]{0:T(128)S(1)} %get-tuple-element.15, f32[128]{0:T(128)S(1)} %get-tuple-element.13), channel_id=1, replica_groups=mesh['row'=16,'col'=16] {'row','col'}, use_global_device_ids=true, to_apply=%region_6.0 | all-reduce | flops 256 | bytes 2048 | tf_op jit(solution)/shard_map/psum | solution.py:43
  97.6 21.1 %all_gather.6 = bf16[256,128]{1,0:T(8,128)(2,1)S(1)} all-gather(bf16[16,128]{1,0:T(8,128)(2,1)S(1)} %get-tuple-element.16), channel_id=1, replica_groups=mesh['row'=16,'col'=16] {'col'}, dimensions={0}, use_global_device_ids=true | all-gather | bytes 69632 | tf_op jit(solution)/shard_map/all_gather | solution.py:39
  118.7 1.3 dynamic-slice
  120.7 0.0 all-to-all-done
  120.7 5.6 multiply_convert_fusion.1
  126.3 0.0 copy-done.2
  126.3 8.1 %fusion.1 = bf16[32768,128]{1,0:T(8,128)(2,1)S(1)} fusion(bf16[32768,128]{1,0:T(8,128)(2,1)} %bitcast.27, bf16[32768,128]{1,0:T(8,128)(2,1)} %bitcast.31, f32[128,128]{1,0:T(8,128)S(1)} %copy-done.2), kind=kOutput, calls=%fused_computation.3 | convolution fusion | flops 1086341120 | bytes 25231360 | tf_op jit(solution)/shard_map/dot_general | solution.py:23
  134.4 0.0 copy-start.1
  134.4 3.2 copy-done.1
  137.6 6.4 fusion.11
  144.0 12.1 %multiply_reduce_fusion.3 = (bf16[256,128]{1,0:T(8,128)(2,1)}, f32[32768,128]{1,0:T(8,128)}) fusion(f32[128,128]{1,0:T(8,128)S(1)} %bitcast_convert_fusion.1, bf16[32768,128]{1,0:T(8,128)(2,1)} %copy-done.1, f32[128,128]{1,0:T(8,128)S(1)} %copy-done.2), kind=kOutput, calls=%fused_computation.8 | convolution fusion | flops 1082114048 | bytes 25362432 | tf_op jit(solution)/shard_map/dot_general | solution.py:25
  156.1 0.0 all-reduce.7.cloned.1.call-update
  156.1 0.0 copy-start.5
  156.1 0.0 copy-start.4
  156.1 7.3 multiply_reduce_fusion.2
  163.4 48.4 %all-reduce = bf16[128,128]{1,0:T(8,128)(2,1)S(1)} all-reduce(bf16[128,128]{1,0:T(8,128)(2,1)S(1)} %multiply_reduce_fusion.2), channel_id=3, replica_groups=mesh['row'=16,'col'=16] {'row'}, use_global_device_ids=true, to_apply=%region_8.0.clone | all-reduce | flops 16384 | bytes 65536
  211.8 183.3 %all-reduce.7.cloned.1.call-done = f32[128,128]{1,0:T(8,128)} async-done(((f32[128,128]{1,0:T(8,128)}), f32[128,128]{1,0:T(8,128)}) %all-reduce.7.cloned.1.call-update) | async-done | bytes 65552 | tf_op jit(solution)/shard_map/psum | solution.py:60
  395.1 0.9 multiply_reduce_fusion.4
  396.0 0.0 copy-done.5
  396.0 0.6 stack.5
  396.7 3.5 all-to-all-start.1
  400.2 0.0 reduce-scatter.3.cloned.1.call-start
  400.2 0.5 reduce-scatter.3.cloned.1.call-update
  400.7 0.0 all-reduce.9.cloned.1.call-start
  400.8 6.7 all-to-all-done.1
  407.5 65.4 %reduce-scatter.3.cloned.1.call-done = bf16[16,128]{1,0:T(8,128)(2,1)} async-done(((bf16[256,128]{1,0:T(8,128)(2,1)}), bf16[16,128]{1,0:T(8,128)(2,1)}) %reduce-scatter.3.cloned.1.call-update) | async-done | bytes 4112 | tf_op jit(solution)/shard_map/reduce_scatter | solution.py:52
  472.9 0.0 copy-done.4
  472.9 0.7 multiply_reduce_fusion.6
  473.6 24.7 %all_gather.7 = bf16[256,128]{1,0:T(8,128)(2,1)S(1)} all-gather(bf16[16,128]{1,0:T(8,128)(2,1)S(1)} %get-tuple-element.10), channel_id=1, replica_groups=mesh['row'=16,'col'=16] {'col'}, dimensions={0}, use_global_device_ids=true | all-gather | bytes 69632 | tf_op jit(solution)/shard_map/all_gather | solution.py:39
  498.4 5.6 multiply_convert_fusion
  504.0 8.1 %fusion = bf16[32768,128]{1,0:T(8,128)(2,1)S(1)} fusion(bf16[32768,128]{1,0:T(8,128)(2,1)} %bitcast.25, bf16[128,128]{1,0:T(8,128)(2,1)S(1)} %get-tuple-element.8, bf16[32768,128]{1,0:T(8,128)(2,1)} %bitcast.32), kind=kOutput, calls=%fused_computation.1 | convolution fusion | flops 1086324736 | bytes 25198592 | tf_op jit(solution)/shard_map/dot_general | solution.py:23
  512.1 0.0 copy-start
  512.1 3.2 copy-done
  515.3 6.4 fusion.12
  521.7 12.1 %multiply_reduce_fusion.1 = (bf16[256,128]{1,0:T(8,128)(2,1)}, f32[32768,128]{1,0:T(8,128)}) fusion(f32[128,128]{1,0:T(8,128)S(1)} %bitcast_convert_fusion, bf16[32768,128]{1,0:T(8,128)(2,1)} %copy-done, bf16[128,128]{1,0:T(8,128)(2,1)S(1)} %get-tuple-element.8), kind=kOutput, calls=%fused_computation.5 | convolution fusion | flops 1082097664 | bytes 25329664 | tf_op jit(solution)/shard_map/dot_general | solution.py:25
  533.8 0.0 all-reduce.9.cloned.1.call-update
  533.8 0.0 reduce-scatter.5.cloned.1.call-start
  533.9 0.0 copy-start.3
  533.9 0.0 copy-start.6
  533.9 7.3 multiply_reduce_fusion
  541.2 49.5 %all-reduce.1 = bf16[128,128]{1,0:T(8,128)(2,1)S(1)} all-reduce(bf16[128,128]{1,0:T(8,128)(2,1)S(1)} %multiply_reduce_fusion), channel_id=5, replica_groups=mesh['row'=16,'col'=16] {'row'}, use_global_device_ids=true, to_apply=%region_18.0.clone | all-reduce | flops 16384 | bytes 65536
  590.7 86.9 %all-reduce.2 = (f32[128]{0:T(128)S(1)}, f32[128]{0:T(128)S(1)}) all-reduce(f32[128]{0:T(128)S(1)} %get-tuple-element.11, f32[128]{0:T(128)S(1)} %get-tuple-element.9), channel_id=1, replica_groups=mesh['row'=16,'col'=16] {'row','col'}, use_global_device_ids=true, to_apply=%region_10.0 | all-reduce | flops 256 | bytes 2048 | tf_op jit(solution)/shard_map/psum | solution.py:43
  677.6 0.6 multiply_add_fusion.4
  678.2 0.0 reduce-scatter.5.cloned.1.call-update
  678.2 95.7 %all-reduce.9.cloned.1.call-done = f32[128,128]{1,0:T(8,128)} async-done(((f32[128,128]{1,0:T(8,128)}), f32[128,128]{1,0:T(8,128)}) %all-reduce.9.cloned.1.call-update) | async-done | bytes 65552 | tf_op jit(solution)/shard_map/psum | solution.py:60
  773.9 0.0 copy-done.3
  773.9 1.5 multiply_add_fusion
  775.4 0.0 reduce-scatter.5.cloned.1.call-done
  775.4 0.0 copy-done.6
  775.4 1.3 multiply_add_fusion.2
  (8 shorter events, 0.1 us)
Async XLA Ops:
  8.0 118.3 %copy-start.2 = (f32[128,128]{1,0:T(8,128)S(1)}, f32[128,128]{1,0:T(8,128)}, u32[]{:S(2)}) copy-start(f32[128,128]{1,0:T(8,128)} %param.7) | copy-start | bytes 196612
  9.4 111.3 %all-to-all-start = ((bf16[16,8,128]{2,1,0:T(8,128)(2,1)}), bf16[16,8,128]{2,1,0:T(8,128)(2,1)S(1)}, u32[]{:S(2)}, u32[]{:S(2)}) async-start(bf16[16,8,128]{2,1,0:T(8,128)(2,1)} %stack.4), calls=%async_computation | async-start | bytes 65536 | tf_op jit(solution)/shard_map/all_to_all | solution.py:41
  19.4 375.7 %all-reduce.7.cloned.1.call-start = ((), (), s32[]{:S(2)}) async-start(), calls=%async_computation.5 | async-start | bytes 131072 | tf_op jit(solution)/shard_map/psum | solution.py:60
  134.4 3.2 copy-start.1
  156.1 239.9 %copy-start.5 = (f32[8,128]{1,0:T(8,128)S(1)}, f32[8,128]{1,0:T(8,128)}, u32[]{:S(2)}) copy-start(f32[8,128]{1,0:T(8,128)} %param.6) | copy-start | bytes 12292
  156.1 316.8 %copy-start.4 = (f32[16,128]{1,0:T(8,128)S(1)}, f32[16,128]{1,0:T(8,128)}, u32[]{:S(2)}) copy-start(f32[16,128]{1,0:T(8,128)} %param.5) | copy-start | bytes 24580
  396.7 10.8 %all-to-all-start.1 = ((bf16[16,8,128]{2,1,0:T(8,128)(2,1)}), bf16[16,8,128]{2,1,0:T(8,128)(2,1)S(1)}, u32[]{:S(2)}, u32[]{:S(2)}) async-start(bf16[16,8,128]{2,1,0:T(8,128)(2,1)} %stack.5), calls=%async_computation.2 | async-start | bytes 65536 | tf_op jit(solution)/shard_map/all_to_all | solution.py:41
  400.2 72.7 %reduce-scatter.3.cloned.1.call-start = ((), (), s32[]{:S(2)}) async-start(), calls=%async_computation.4 | async-start | bytes 69632 | tf_op jit(solution)/shard_map/reduce_scatter | solution.py:52
  400.7 373.2 %all-reduce.9.cloned.1.call-start = ((), (), s32[]{:S(2)}) async-start(), calls=%async_computation.7 | async-start | bytes 131072 | tf_op jit(solution)/shard_map/psum | solution.py:60
  512.1 3.2 copy-start
  533.8 241.6 %reduce-scatter.5.cloned.1.call-start = ((), (), s32[]{:S(2)}) async-start(), calls=%async_computation.6 | async-start | bytes 69632 | tf_op jit(solution)/shard_map/reduce_scatter | solution.py:52
  533.9 240.0 %copy-start.3 = (f32[128,128]{1,0:T(8,128)S(1)}, f32[128,128]{1,0:T(8,128)}, u32[]{:S(2)}) copy-start(f32[128,128]{1,0:T(8,128)} %all-reduce.7.cloned.1.call-done) | copy-start | bytes 196612
  533.9 241.5 %copy-start.6 = (bf16[16,128]{1,0:T(8,128)(2,1)S(1)}, bf16[16,128]{1,0:T(8,128)(2,1)}, u32[]{:S(2)}) copy-start(bf16[16,128]{1,0:T(8,128)(2,1)} %reduce-scatter.3.cloned.1.call-done) | copy-start | bytes 12292
Sparse Core Ops, SparseCore 0:
  156.2 238.8 all-reduce.6
  533.9 239.9 all-reduce.8
Sparse Core Ops, SparseCore 1:
  405.1 67.8 reduce-scatter.2
  678.3 61.0 reduce-scatter.4
